TPU v7x, 32 devices: a whole 2x2x4 slice. The times are simulated.
32 devices in a mesh: dp: 4 (over z), seq: 2 (over y), mp: 4 (over x, core).
Axes of the slice: x: 2, y: 2, z: 4, core: 2. Of those that a mesh axis runs over, the one named last changes fastest.
Arguments:
- hidden_in: bfloat16 [4, 1024, 768], P('dp', 'seq', 'mp'), may hold values from -6 to 6
- cotangent: bfloat16 [4, 1024, 768], P('dp', 'seq', 'mp'), may hold values from -6 to 6
- attention_gain: float32 [768], replicated, may hold values from 0.1 to 1.9
- feedforward_gain: float32 [768], replicated, may hold values from 0.1 to 1.9
- qkv_weight: bfloat16 [768, 3, 768], P(None, None, 'mp'), may hold values from -0.21875 to 0.21875
- attention_out: bfloat16 [768, 768], P('mp'), may hold values from -0.75 to 0.75
- geglu_in: bfloat16 [768, 2, 1152], P(None, None, 'mp'), may hold values from -0.21875 to 0.21875
- geglu_out: bfloat16 [1152, 768], P('mp'), may hold values from -0.1875 to 0.1875
Outputs:
- layer_out: float32 [4, 1024, 768], P('dp', 'seq', 'mp')
- grad_input: float32 [4, 1024, 768], P('dp', 'seq', 'mp')
- grad_qkv: float32 [768, 3, 768], P(None, None, 'mp')
- grad_attention_out: float32 [768, 768], P('mp')
- grad_geglu_in: float32 [768, 2, 1152], P(None, None, 'mp')
- grad_geglu_out: float32 [1152, 768], P('mp')
- grad_attention_gain: float32 [768], P('mp')
- grad_feedforward_gain: float32 [768], P('mp')
All inputs are finite; a program needn't handle non-finite values.
Results may differ from a plain program's by a relative error of at most 0.018.
Values may be sent and summed in bfloat16 or wider, within the bound.
No kernel may reach another device: no remote copies, remote signals or barrier semaphores. Data moves between devices by JAX's collectives and lax.ppermute only.
A program may use at most 64 MiB of HBM per device.

v0:
```python
import math
import jax
import jax.numpy as jnp
from jax import lax
from jax.sharding import PartitionSpec as P

HEAD = 64
HALF = 64


def with_halo(block, sides, width):
    for axis, dim in sides:
        count = lax.axis_size(axis)
        forward = [(i, i + 1) for i in range(count - 1)]
        backward = [(target, source) for source, target in forward]
        low = lax.ppermute(
            lax.slice_in_dim(block, block.shape[dim] - width, None, axis=dim), axis, forward
        )
        high = lax.ppermute(lax.slice_in_dim(block, 0, width, axis=dim), axis, backward)
        block = jnp.concatenate([low, block, high], axis=dim)
    return block


def normalize(rows):
    center = rows - jnp.mean(rows, axis=-1, keepdims=True)
    inverse = lax.rsqrt(jnp.mean(center * center, axis=-1, keepdims=True) + 1e-05)
    return (center * inverse, inverse)


def frequencies(positions):
    inverse_freq = jnp.exp(
        jnp.arange(HEAD // 2).astype(jnp.float32) * (-2.0 * math.log(10000.0) / HEAD)
    )
    angles = positions[:, None] * inverse_freq[None, :]
    angles = jnp.concatenate([angles, angles], axis=-1)
    return (jnp.cos(angles), jnp.sin(angles))


def rotate(tensor, cosine, sine):
    halfway = HEAD // 2
    turned = jnp.concatenate([-tensor[..., halfway:], tensor[..., :halfway]], axis=-1)
    return tensor * cosine[:, None, :] + turned * sine[:, None, :]


def gelu_exact(value):
    return 0.5 * value * (1.0 + lax.erf(value * 0.7071067811865476))


def gelu_slope(value):
    return (
        0.5 * (1.0 + lax.erf(value * 0.7071067811865476))
        + value * jnp.exp(-0.5 * value * value) * 0.3989422804014327
    )


def windows(wide, tile):
    count = (wide.shape[1] - tile) // tile
    shape = (wide.shape[0], count, tile) + wide.shape[2:]
    lower = wide[:, : count * tile].reshape(shape)
    upper = wide[:, tile:].reshape(shape)
    return jnp.concatenate([lower, upper], axis=2)


def unwindow(grads, tile):
    rest = grads.shape[3:]
    shape = (grads.shape[0], grads.shape[1] * tile) + rest
    lower = grads[:, :, :tile].reshape(shape)
    upper = grads[:, :, tile:].reshape(shape)
    others = ((0, 0),) * len(rest)
    return jnp.pad(lower, ((0, 0), (0, tile)) + others) + jnp.pad(
        upper, ((0, 0), (tile, 0)) + others
    )


def band_mask(base, count, tile, total_length):
    query_off = jnp.arange(tile, dtype=jnp.int32)
    key_off = jnp.arange(2 * tile, dtype=jnp.int32) - HALF
    near = jnp.abs(query_off[:, None] - key_off[None, :]) <= HALF
    key_pos = (
        base
        - HALF
        + jnp.arange(count, dtype=jnp.int32)[:, None] * tile
        + jnp.arange(2 * tile, dtype=jnp.int32)[None, :]
    )
    inside = (key_pos >= 0) & (key_pos < total_length)
    return near[None] & inside[:, None, :]


def attend(queries, keys_wide, values_wide, allowed):
    batch, length, heads, size = queries.shape
    tile = 2 * HALF
    count = length // tile
    query_tiles = queries.reshape(batch, count, tile, heads, size)
    key_tiles = windows(keys_wide, tile)
    value_tiles = windows(values_wide, tile)
    scores = jnp.einsum(
        "snqhd,snkhd->snhqk", query_tiles, key_tiles, preferred_element_type=jnp.float32
    ) * HEAD ** (-0.5)
    scores = jnp.where(allowed[None, :, None], scores, -1e30)
    top = jnp.max(scores, axis=-1, keepdims=True)
    log_total = top + jnp.log(jnp.sum(jnp.exp(scores - top), axis=-1, keepdims=True))
    weights = jnp.exp(scores - log_total).astype(jnp.bfloat16)
    mixed = jnp.einsum(
        "snhqk,snkhd->snqhd", weights, value_tiles, preferred_element_type=jnp.float32
    ).astype(jnp.bfloat16)
    return (mixed.reshape(batch, length, heads, size), log_total)


def attend_back(queries, keys_wide, values_wide, allowed, log_total, mixed, grad_mixed):
    batch, length, heads, size = queries.shape
    tile = 2 * HALF
    count = length // tile
    query_tiles = queries.reshape(batch, count, tile, heads, size)
    key_tiles = windows(keys_wide, tile)
    value_tiles = windows(values_wide, tile)
    grad_tiles = grad_mixed.reshape(batch, count, tile, heads, size)
    again = jnp.einsum(
        "snqhd,snkhd->snhqk", query_tiles, key_tiles, preferred_element_type=jnp.float32
    ) * HEAD ** (-0.5)
    again = jnp.where(allowed[None, :, None], again, -1e30)
    probs = jnp.exp(again - log_total)
    delta = jnp.sum(grad_mixed.astype(jnp.float32) * mixed.astype(jnp.float32), axis=-1)
    delta = jnp.transpose(delta.reshape(batch, count, tile, heads), (0, 1, 3, 2))
    grad_value_tiles = jnp.einsum(
        "snhqk,snqhd->snkhd",
        probs.astype(jnp.bfloat16),
        grad_tiles,
        preferred_element_type=jnp.float32,
    )
    grad_probs = jnp.einsum(
        "snqhd,snkhd->snhqk", grad_tiles, value_tiles, preferred_element_type=jnp.float32
    )
    grad_scores = (probs * (grad_probs - delta[..., None]) * HEAD ** (-0.5)).astype(jnp.bfloat16)
    grad_queries = jnp.einsum(
        "snhqk,snkhd->snqhd", grad_scores, key_tiles, preferred_element_type=jnp.float32
    )
    grad_key_tiles = jnp.einsum(
        "snhqk,snqhd->snkhd", grad_scores, query_tiles, preferred_element_type=jnp.float32
    )
    return (
        grad_queries.reshape(batch, length, heads, size),
        unwindow(grad_key_tiles, tile),
        unwindow(grad_value_tiles, tile),
    )


def edge_rims(grad_packed, length):
    return jnp.concatenate([grad_packed[:, :HALF], grad_packed[:, HALF + length :]], axis=1)


def fold_rims(grad_packed, returned, length):
    lower_add = jnp.pad(returned[:, :HALF], ((0, 0), (0, length - HALF), (0, 0)))
    upper_add = jnp.pad(returned[:, 3 * HALF :], ((0, 0), (length - HALF, 0), (0, 0)))
    return grad_packed[:, HALF : HALF + length] + lower_add + upper_add


def body(
    hidden_in,
    cotangent,
    attention_gain,
    feedforward_gain,
    qkv_weight,
    attention_out,
    geglu_in,
    geglu_out,
):
    batch, length, share = hidden_in.shape
    width = share * lax.axis_size("mp")
    offset = lax.axis_index("mp") * share
    columns = qkv_weight.shape[2]
    heads = columns // HEAD
    span = length + 2 * HALF
    inputs_full, upstream_full = (
        lax.all_gather(hidden_in, "mp", axis=2, tiled=True),
        lax.all_gather(cotangent, "mp", axis=2, tiled=True),
    )
    normed_one, inverse_one = normalize(inputs_full.astype(jnp.float32))
    fed_one = (normed_one * attention_gain).astype(jnp.bfloat16)
    projected = jnp.einsum("std,dch->stch", fed_one, qkv_weight, preferred_element_type=jnp.float32)
    block_index = lax.axis_index("seq")
    total_length = length * lax.axis_size("seq")
    query_pos = block_index * length + jnp.arange(length, dtype=jnp.int32)
    cosine, sine = frequencies(query_pos.astype(jnp.float32))
    queries = rotate(projected[:, :, 0].reshape(batch, length, heads, HEAD), cosine, sine).astype(
        jnp.bfloat16
    )
    keys_own = rotate(projected[:, :, 1].reshape(batch, length, heads, HEAD), cosine, sine).astype(
        jnp.bfloat16
    )
    values_own = projected[:, :, 2].astype(jnp.bfloat16)
    packed = jnp.concatenate([keys_own.reshape(batch, length, columns), values_own], axis=2)
    widened = with_halo(packed, (("seq", 1),), HALF)
    keys_wide = widened[:, :, :columns].reshape(batch, span, heads, HEAD)
    values_wide = widened[:, :, columns:].reshape(batch, span, heads, HEAD)
    allowed = band_mask(block_index * length, length // (2 * HALF), 2 * HALF, total_length)
    mixed, log_total = attend(queries, keys_wide, values_wide, allowed)
    joined = mixed.reshape(batch, length, columns)
    attn_terms = jnp.einsum(
        "sqh,hd->sqd", joined, attention_out, preferred_element_type=jnp.float32
    )
    middle = hidden_in.astype(jnp.float32) + lax.psum_scatter(
        attn_terms, "mp", scatter_dimension=2, tiled=True
    )
    middle_full = lax.all_gather(middle, "mp", axis=2, tiled=True)
    normed_two, inverse_two = normalize(middle_full)
    fed_two = (normed_two * feedforward_gain).astype(jnp.bfloat16)
    lifted = jnp.einsum("std,dcf->stcf", fed_two, geglu_in, preferred_element_type=jnp.float32)
    linear = lifted[:, :, 0]
    gating = lifted[:, :, 1]
    activated = gelu_exact(linear)
    product = (activated * gating).astype(jnp.bfloat16)
    mlp_terms = jnp.einsum("stf,fd->std", product, geglu_out, preferred_element_type=jnp.float32)
    layer_out = middle + lax.psum_scatter(
        mlp_terms.astype(jnp.bfloat16), "mp", scatter_dimension=2, tiled=True
    ).astype(jnp.float32)
    grad_geglu_out = jnp.einsum(
        "stf,std->fd", product, upstream_full, preferred_element_type=jnp.float32
    )
    grad_product = jnp.einsum(
        "std,fd->stf", upstream_full, geglu_out, preferred_element_type=jnp.float32
    )
    grad_linear = grad_product * gating * gelu_slope(linear)
    grad_gating = grad_product * activated
    grad_lifted = jnp.stack([grad_linear, grad_gating], axis=2).astype(jnp.bfloat16)
    grad_geglu_in = jnp.einsum(
        "std,stcf->dcf", fed_two, grad_lifted, preferred_element_type=jnp.float32
    )
    fed_terms = jnp.einsum(
        "stcf,dcf->std", grad_lifted, geglu_in, preferred_element_type=jnp.float32
    )
    grad_fed_two = lax.psum_scatter(fed_terms, "mp", scatter_dimension=2, tiled=True)
    normed_two_own = lax.dynamic_slice_in_dim(normed_two, offset, share, 2)
    gain_two_own = lax.dynamic_slice_in_dim(feedforward_gain, offset, share, 0)
    grad_ff_gain = jnp.sum(grad_fed_two * normed_two_own, axis=(0, 1))
    dhat_two = grad_fed_two * gain_two_own
    first_two, second_two = lax.psum(
        (
            jnp.sum(dhat_two, axis=-1, keepdims=True),
            jnp.sum(dhat_two * normed_two_own, axis=-1, keepdims=True),
        ),
        "mp",
    )
    grad_middle = cotangent.astype(jnp.float32) + inverse_two * (
        dhat_two - first_two / width - normed_two_own * (second_two / width)
    )
    grad_middle_full = lax.all_gather(grad_middle.astype(jnp.bfloat16), "mp", axis=2, tiled=True)
    grad_attention_out = jnp.einsum(
        "sqh,sqd->hd", joined, grad_middle_full, preferred_element_type=jnp.float32
    )
    grad_mixed = jnp.einsum(
        "sqd,hd->sqh", grad_middle_full, attention_out, preferred_element_type=jnp.float32
    ).astype(jnp.bfloat16)
    grad_mixed = grad_mixed.reshape(batch, length, heads, HEAD)
    grad_queries, grad_keys_wide, grad_values_wide = attend_back(
        queries, keys_wide, values_wide, allowed, log_total, mixed, grad_mixed
    )
    grad_packed = jnp.concatenate(
        [
            grad_keys_wide.reshape(batch, span, columns),
            grad_values_wide.reshape(batch, span, columns),
        ],
        axis=2,
    )
    returned = with_halo(
        edge_rims(grad_packed, length).astype(jnp.bfloat16), (("seq", 1),), HALF
    ).astype(jnp.float32)
    grad_own = fold_rims(grad_packed, returned, length)
    grad_keys = rotate(grad_own[:, :, :columns].reshape(batch, length, heads, HEAD), cosine, -sine)
    grad_queries = rotate(grad_queries, cosine, -sine)
    grad_values = grad_own[:, :, columns:].reshape(batch, length, heads, HEAD)
    grad_projected = (
        jnp.stack([grad_queries, grad_keys, grad_values], axis=2)
        .reshape(batch, length, 3, columns)
        .astype(jnp.bfloat16)
    )
    grad_qkv = jnp.einsum(
        "std,stch->dch", fed_one, grad_projected, preferred_element_type=jnp.float32
    )
    one_terms = jnp.einsum(
        "stch,dch->std", grad_projected, qkv_weight, preferred_element_type=jnp.float32
    )
    grad_fed_one = lax.psum_scatter(
        one_terms.astype(jnp.bfloat16), "mp", scatter_dimension=2, tiled=True
    ).astype(jnp.float32)
    normed_one_own = lax.dynamic_slice_in_dim(normed_one, offset, share, 2)
    gain_one_own = lax.dynamic_slice_in_dim(attention_gain, offset, share, 0)
    grad_attn_gain = jnp.sum(grad_fed_one * normed_one_own, axis=(0, 1))
    dhat_one = grad_fed_one * gain_one_own
    first_one, second_one = lax.psum(
        (
            jnp.sum(dhat_one, axis=-1, keepdims=True),
            jnp.sum(dhat_one * normed_one_own, axis=-1, keepdims=True),
        ),
        "mp",
    )
    grad_input = grad_middle + inverse_one * (
        dhat_one - first_one / width - normed_one_own * (second_one / width)
    )
    local_grads = (
        grad_qkv,
        grad_attention_out,
        grad_geglu_in,
        grad_geglu_out,
        grad_attn_gain,
        grad_ff_gain,
    )
    summed = lax.psum(
        (
            local_grads[0],
            local_grads[1],
            local_grads[2],
            local_grads[3],
            local_grads[4],
            local_grads[5],
        ),
        ("dp", "seq"),
    )
    return (layer_out, grad_input, summed[0], summed[1], summed[2], summed[3], summed[4], summed[5])


def solution(mesh):
    in_specs = (
        P("dp", "seq", "mp"),
        P("dp", "seq", "mp"),
        P(),
        P(),
        P(None, None, "mp"),
        P("mp", None),
        P(None, None, "mp"),
        P("mp", None),
    )
    out_specs = (
        P("dp", "seq", "mp"),
        P("dp", "seq", "mp"),
        P(None, None, "mp"),
        P("mp", None),
        P(None, None, "mp"),
        P("mp", None),
        P("mp"),
        P("mp"),
    )
    return jax.shard_map(body, mesh=mesh, in_specs=in_specs, out_specs=out_specs, check_vma=False)
```

profile of v0, /device:TPU:0, one launch (start us, length us, event | category | flops | bytes accessed | tf_op | source)
XLA Modules:
  0.0 433.2 jit_solution(13001490404904794870)
XLA Ops:
  7.3 10.4 %all_gather.12 = bf16[1,512,768]{1,2,0:T(8,128)(2,1)S(1)} all-gather(bf16[1,512,192]{1,2,0:T(8,128)(2,1)} %param.8), channel_id=1, replica_groups=mesh['dp'=4,'seq'=2,'mp'=4] {'mp'}, dimensions={2}, use_global_device_ids=true | all-gather | bytes 983040 | tf_op jit(solution)/shard_map/all_gather | solution.py:174
  18.1 0.7 fusion.78
  18.9 1.0 copy-done.17
  20.0 0.9 fusion.85
  21.0 1.1 fusion.46
  22.1 0.7 pad_maximum_fusion.12
  22.8 3.4 collective-permute-start
  26.2 1.3 collective-permute-start.1
  27.8 1.7 fusion.81
  29.7 0.7 slice_negate_fusion.2
  30.4 1.0 concatenate.132
  31.4 1.1 fusion.43
  33.0 1.2 pad_maximum_fusion.2
  37.7 2.7 copy.56
  42.3 43.4 %all-reduce.16.cloned.1.call-done = f32[1,512,768]{1,0,2:T(1,128)} async-done(((f32[1,512,768]{1,0,2:T(1,128)}), f32[1,512,768]{1,0,2:T(1,128)}) %all-reduce.16.cloned.1.call-update) | async-done | bytes 1572880
  85.7 2.1 dynamic-slice_add_fusion
  87.9 8.6 %all_gather.14 = bf16[1,512,768]{1,2,0:T(8,128)(2,1)} all-gather(bf16[1,512,192]{1,2,0:T(8,128)(2,1)S(1)} %copy-done.12), channel_id=1, replica_groups=mesh['dp'=4,'seq'=2,'mp'=4] {'mp'}, dimensions={2}, use_global_device_ids=true | all-gather | bytes 983040 | tf_op jit(solution)/shard_map/all_gather | solution.py:175
  96.5 11.2 %all-gather.2.cloned.1.call-done = f32[1,512,768]{1,0,2:T(1,128)} async-done(((f32[1,512,192]{1,0,2:T(1,128)}), f32[1,512,768]{1,0,2:T(1,128)}) %all-gather.2.cloned.1.call-update) | async-done | bytes 1572880 | tf_op jit(solution)/shard_map/all_gather | solution.py:204
  107.7 2.4 reduce_sum.111
  110.4 1.1 copy-done.4
  111.8 1.0 copy-done.22
  112.7 0.7 convolution_bitcast_fusion.2
  115.0 0.7 copy-done.42
  115.8 2.0 convolution_bitcast_fusion
  117.8 4.8 %copy.60 = f32[1,512,768]{1,0,2:T(1,128)} copy(f32[1,512,768]{2,1,0:T(8,128)} %convolution_bitcast_fusion) | data formatting | bytes 3145728 | tf_op jit(solution)/shard_map/stcf,dcf->std/dot_general | solution.py:228
  122.7 0.9 copy.63
  123.6 2.9 fusion.6
  126.6 4.8 %copy.86 = bf16[1,512,768]{1,0,2:T(2,128)(2,1)} copy(bf16[1,512,768]{2,1,0:T(8,128)(2,1)} %fusion.6) | data formatting | bytes 1572864
  131.3 2.5 copy.151
  133.9 31.7 %all-reduce.18.cloned.1.call-done = f32[1,512,768]{1,0,2:T(1,128)} async-done(((f32[1,512,768]{1,0,2:T(1,128)}), f32[1,512,768]{1,0,2:T(1,128)}) %all-reduce.18.cloned.1.call-update) | async-done | bytes 1572880
  165.6 1.3 constant_dynamic-slice_fusion
  166.9 0.8 copy-done.7
  167.8 6.0 %all-reduce.11 = (f32[1,512,1]{1,2,0:T(1,128)S(1)}, f32[1,512,1]{1,2,0:T(1,128)S(1)}) all-reduce(f32[1,512,1]{1,2,0:T(1,128)S(1)} %bitcast.303, f32[1,512,1]{1,2,0:T(1,128)S(1)} %bitcast.304), channel_id=1, replica_groups=mesh['dp'=4,'seq'=2,'mp'=4] {'mp'}, use_global_device_ids=true, to_apply=%region_12.13 | all-reduce | flops 1024 | bytes 8192 | tf_op jit(solution)/shard_map/psum | solution.py:236
  173.8 1.2 fusion.98
  175.0 8.3 %all_gather.15 = bf16[1,512,768]{1,2,0:T(8,128)(2,1)S(1)} all-gather(bf16[1,512,192]{1,2,0:T(8,128)(2,1)S(1)} %fusion.98), channel_id=1, replica_groups=mesh['dp'=4,'seq'=2,'mp'=4] {'mp'}, dimensions={2}, use_global_device_ids=true | all-gather | bytes 983040 | tf_op jit(solution)/shard_map/all_gather | solution.py:246
  183.3 0.9 copy-done.5
  184.6 0.7 reshape.839
  185.3 1.6 fusion.47
  187.0 2.1 convolution_bitcast_fusion.3
  193.4 3.4 collective-permute-start.2
  196.8 1.3 collective-permute-start.3
  199.4 4.1 collective-permute-done.3
  204.3 0.7 copy-done.41
  206.1 1.7 fusion.5
  207.9 4.8 %copy.88 = bf16[1,512,768]{1,0,2:T(2,128)(2,1)} copy(bf16[1,512,768]{2,1,0:T(8,128)(2,1)} %fusion.5) | data formatting | bytes 1572864
  212.6 2.5 copy.150
  215.2 2.9 fusion.16
  218.1 1.9 fusion.48
  220.1 1.2 fusion.13
  221.4 2.0 fusion.76
  223.5 1.4 fusion
  224.9 1.4 fusion.44
  226.3 0.8 copy.79
  227.1 10.6 %reduce-scatter.9.cloned.1.call-done = bf16[192,512]{1,0:T(8,128)(2,1)} async-done(((bf16[768,512]{1,0:T(8,128)(2,1)}), bf16[192,512]{1,0:T(8,128)(2,1)}) %reduce-scatter.9.cloned.1.call-update) | async-done | bytes 196624
  237.7 1.1 reshape_bitcast_fusion
  238.8 1.2 fusion.37
  240.0 22.6 %all-reduce.8 = (f32[192]{0:T(256)}, f32[192]{0:T(256)}) all-reduce(f32[192]{0:T(256)S(1)} %get-tuple-element.34, f32[192]{0:T(256)S(1)} %get-tuple-element.32), channel_id=1, replica_groups=mesh['dp'=4,'seq'=2,'mp'=4] {'dp','seq'}, use_global_device_ids=true, to_apply=%region_24.25 | all-reduce | flops 384 | bytes 3072 | tf_op jit(solution)/shard_map/psum | solution.py:307
  262.6 6.0 %all-reduce.10 = (f32[1,512,1]{1,2,0:T(1,128)S(1)}, f32[1,512,1]{1,2,0:T(1,128)S(1)}) all-reduce(f32[1,512,1]{1,2,0:T(1,128)S(1)} %bitcast.301, f32[1,512,1]{1,2,0:T(1,128)S(1)} %bitcast.302), channel_id=1, replica_groups=mesh['dp'=4,'seq'=2,'mp'=4] {'mp'}, use_global_device_ids=true, to_apply=%region_18.19 | all-reduce | flops 1024 | bytes 8192 | tf_op jit(solution)/shard_map/psum | solution.py:289
  268.7 2.0 fusion.35
  270.7 149.2 %all-reduce.20.cloned.1.call-done = (f32[768,3,192]{0,2,1:T(8,128)}, f32[192,768]{1,0:T(8,128)}, f32[768,2,288]{0,2,1:T(8,128)}, f32[288,768]{1,0:T(8,128)}) async-done(((f32[768,3,192]{0,2,1:T(8,128)}, f32[192,768]{1,0:T(8,128)}, f32[768,2,288]{0,2,1:T(8,128)}, f32[288,768]{1,0:T(8,128)}), (f32[768,3,192]{0,2,1:T(8,128)}, f32[192,768]{1,0:T(8,128)}, f32[768,2,288]{0,2,1:T(8,128)}, ...) | async-done | bytes 5013520 | tf_op jit(solution)/shard_map/psum | solution.py:307
  419.9 2.9 copy.158
  422.8 0.8 copy.159
  423.7 1.2 copy.160
  425.4 0.9 copy.161
  (187 shorter events, 17.0 us)
Async XLA Ops:
  7.2 10.9 %copy-start = (bf16[768,3,192]{0,2,1:T(8,128)(2,1)S(1)}, bf16[768,3,192]{0,2,1:T(8,128)(2,1)}, u32[]{:S(2)}) copy-start(bf16[768,3,192]{0,2,1:T(8,128)(2,1)} %param.12) | copy-start | bytes 2654212
  7.2 10.9 %copy-start.47 = (f32[768]{0:T(1024)S(1)}, f32[768]{0:T(1024)}, u32[]{:S(2)}) copy-start(f32[768]{0:T(1024)} %param.10) | copy-start | bytes 9220
  7.2 78.5 %all-reduce.16.cloned.1.call-start = ((), (), s32[]{:S(2)}) async-start(), calls=%async_computation.5 | async-start | bytes 3145728
  18.8 1.0 copy-start.17
  20.9 1.9 copy-start.18
  22.8 9.8 %collective-permute-start = (bf16[1,64,384]{1,2,0:T(8,128)(2,1)}, bf16[1,64,384]{1,2,0:T(8,128)(2,1)S(1)}, u32[]{:S(2)}, u32[]{:S(2)}) collective-permute-start(bf16[1,64,384]{1,2,0:T(8,128)(2,1)} %get-tuple-element.71), channel_id=1, source_target_pairs={{0,4},{1,5},{2,6},{3,7},{8,12},{9,13},{10,14},{11,15},{16,20},{17,... | collective-permute-start | bytes 147464 | tf_op jit(solution)/shard_map/ppermute | solution.py:16
  26.2 6.8 %collective-permute-start.1 = (bf16[1,64,384]{1,2,0:T(8,128)(2,1)S(1)}, bf16[1,64,384]{1,2,0:T(8,128)(2,1)}, u32[]{:S(2)}, u32[]{:S(2)}) collective-permute-start(bf16[1,64,384]{1,2,0:T(8,128)(2,1)S(1)} %get-tuple-element.72), channel_id=1, source_target_pairs={{4,0},{5,1},{6,2},{7,3},{12,8},{13,9},{14,10},{15,11},{20,16},{21,... | collective-permute-start | bytes 147464 | tf_op jit(solution)/shard_map/ppermute | solution.py:19
  32.6 1.9 copy-start.24
  34.5 0.7 copy-start.27
  34.5 0.7 copy-start.29
  35.1 1.2 copy-start.1
  35.8 1.5 copy-start.20
  35.9 0.7 copy-start.31
  35.9 0.7 copy-start.33
  36.6 0.7 copy-start.15
  40.4 0.7 copy-start.49
  40.4 45.3 %copy-start.35 = (bf16[1,512,192]{1,2,0:T(8,128)(2,1)S(1)}, bf16[1,512,192]{1,2,0:T(8,128)(2,1)}, u32[]{:S(2)}) copy-start(bf16[1,512,192]{1,2,0:T(8,128)(2,1)} %param.8) | copy-start | bytes 589828
  40.4 47.5 %copy-start.12 = (bf16[1,512,192]{1,2,0:T(8,128)(2,1)S(1)}, bf16[1,512,192]{1,2,0:T(8,128)(2,1)}, u32[]{:S(2)}) copy-start(bf16[1,512,192]{1,2,0:T(8,128)(2,1)} %param.9) | copy-start | bytes 589828
  40.5 67.3 %all-gather.2.cloned.1.call-start = ((), (), s32[]{:S(2)}) async-start(), calls=%async_computation.2 | async-start | bytes 1966080 | tf_op jit(solution)/shard_map/all_gather | solution.py:204
  87.9 77.7 %all-reduce.18.cloned.1.call-start = ((), (), s32[]{:S(2)}) async-start(), calls=%async_computation.6 | async-start | bytes 3145728
  107.7 2.4 copy-start.3
  110.1 1.4 copy-start.4
  111.5 1.2 copy-start.22
  111.5 1.2 copy-start.46
  112.7 1.1 copy-start.9
  112.7 1.2 copy-start.48
  114.0 1.0 copy-start.10
  115.0 0.8 copy-start.42
  115.0 0.8 copy-start.44
  122.6 102.3 %reduce-scatter.7.cloned.1.call-start = ((), (), s32[]{:S(2)}) async-start(), calls=%async_computation.3 | async-start | bytes 983040
  133.8 40.0 %copy-start.13 = (bf16[1,512,192]{1,2,0:T(8,128)(2,1)S(1)}, bf16[1,512,192]{1,2,0:T(8,128)(2,1)}, u32[]{:S(2)}) copy-start(bf16[1,512,192]{1,2,0:T(8,128)(2,1)} %param.9) | copy-start | bytes 589828
  133.9 103.9 %reduce-scatter.9.cloned.1.call-start = ((), (), s32[]{:S(2)}) async-start(), calls=%async_computation.4 | async-start | bytes 983040
  166.9 0.8 copy-start.7
  173.8 10.4 %copy-start.21 = (bf16[192,768]{1,0:T(8,128)(2,1)S(1)}, bf16[192,768]{1,0:T(8,128)(2,1)}, u32[]{:S(2)}) copy-start(bf16[192,768]{1,0:T(8,128)(2,1)} %param.13) | copy-start | bytes 884740
  183.3 0.9 copy-start.5
  185.3 3.8 copy-start.26
  187.0 2.2 copy-start.2
  187.0 2.2 copy-start.32
  187.0 2.2 copy-start.34
  189.2 0.9 copy-start.28
  189.2 1.0 copy-start.30
  189.2 1.4 copy-start.25
  193.4 5.9 %collective-permute-start.2 = (bf16[1,64,384]{1,2,0:T(8,128)(2,1)S(1)}, bf16[1,64,384]{1,2,0:T(8,128)(2,1)S(1)}, u32[]{:S(2)}, u32[]{:S(2)}) collective-permute-start(bf16[1,64,384]{1,2,0:T(8,128)(2,1)S(1)} %get-tuple-element.53), channel_id=1, source_target_pairs={{0,4},{1,5},{2,6},{3,7},{8,12},{9,13},{10,14},{11,15},{16,20},{17,... | collective-permute-start | bytes 147464 | tf_op jit(solution)/shard_map/ppermute | solution.py:16
  196.8 6.7 %collective-permute-start.3 = (bf16[1,64,384]{1,2,0:T(8,128)(2,1)S(1)}, bf16[1,64,384]{1,2,0:T(8,128)(2,1)S(1)}, u32[]{:S(2)}, u32[]{:S(2)}) collective-permute-start(bf16[1,64,384]{1,2,0:T(8,128)(2,1)S(1)} %get-tuple-element.54), channel_id=1, source_target_pairs={{4,0},{5,1},{6,2},{7,3},{12,8},{13,9},{14,10},{15,11},{20,16},{21,... | collective-permute-start | bytes 147464 | tf_op jit(solution)/shard_map/ppermute | solution.py:19
  204.1 0.9 copy-start.41
  204.1 1.0 copy-start.19
  205.4 0.7 copy-start.36
  205.4 0.7 copy-start.38
  215.1 204.8 %all-reduce.20.cloned.1.call-start = ((), (), s32[]{:S(2)}) async-start(), calls=%async_computation.7 | async-start | bytes 10027008 | tf_op jit(solution)/shard_map/psum | solution.py:307
  215.2 2.9 copy-start.43
  215.2 2.9 copy-start.45
  218.1 2.0 copy-start.6
  218.1 2.0 copy-start.16
  220.1 1.3 copy-start.37
  220.1 1.3 copy-start.39
  224.9 43.8 %copy-start.8 = (f32[1,512,192]{1,0,2:T(1,128)S(1)}, f32[1,512,192]{1,0,2:T(1,128)}, u32[]{:S(2)}) copy-start(f32[1,512,192]{1,0,2:T(1,128)} %copy-done.7) | copy-start | bytes 1179652
  224.9 43.8 %copy-start.14 = (bf16[1,512,192]{1,2,0:T(8,128)(2,1)S(1)}, bf16[1,512,192]{1,2,0:T(8,128)(2,1)}, u32[]{:S(2)}) copy-start(bf16[1,512,192]{1,2,0:T(8,128)(2,1)} %param.9) | copy-start | bytes 589828
  419.9 3.0 copy-start.40
  419.9 3.8 copy-start.11
  423.7 1.8 copy-start.23
Sparse Core Ops, SparseCore 0:
  40.6 45.0 all-reduce.15
  88.0 19.6 all-gather.1
  122.7 42.8 all-reduce.17
  168.0 23.2 reduce-scatter.6
  215.3 22.4 reduce-scatter.8
  242.1 177.7 all-reduce.19
where the time goes:
time: 434 us; the launch traced here: 433 us
  waiting for transfers between devices  251 us (58%)
  blocking collectives  61.9 us (14%)
  local copies, waits for them, and re-layouts  47.5 us (11%)
  other arithmetic  25.6 us (6%)
  matrix products  21.8 us (5%)
  between operations  15.6 us (4%)
  starting transfers between devices  9.63 us (2%)
    psum x1, waiting for transfers between devices, body(): lax.psum((local_grads[0], local_grads[1], local_grads[2], local_grads[3],...  149 us
    unnamed x10, waiting for transfers between devices  85.8 us
    unnamed x117, local copies, waits for them, and re-layouts  34.8 us
    psum x1, blocking collectives, body(): lax.psum((local_grads[0], local_grads[1], local_grads[2], local_grads[3],...  22.6 us
    all_gather x1, waiting for transfers between devices, body(): middle_full = lax.all_gather(middle, 'mp', axis=2, tiled=True)  11.2 us
    all_gather x1, blocking collectives, body(): lax.all_gather(hidden_in, 'mp', axis=2, tiled=True)  10.4 us
  transfers between devices with their start and end apart: 10, of which 8 were waited for; matrix products, arithmetic and copies ran while one was open for 13% of the time, Pallas kernels for 0%

commit v1 on v0

--- a/solution.py
+++ b/solution.py
@@ -304,17 +304,16 @@
         grad_attn_gain,
         grad_ff_gain,
     )
-    summed = lax.psum(
-        (
-            local_grads[0],
-            local_grads[1],
-            local_grads[2],
-            local_grads[3],
-            local_grads[4],
-            local_grads[5],
-        ),
-        ("dp", "seq"),
-    )
+    summed = (
+        local_grads[0],
+        local_grads[1],
+        local_grads[2],
+        local_grads[3],
+        local_grads[4],
+        local_grads[5],
+    )
+    for w in ("seq", "dp"):
+        summed = lax.psum(summed, axis_name=w)
     return (layer_out, grad_input, summed[0], summed[1], summed[2], summed[3], summed[4], summed[5])
 
 

time: 434 us -> 582 us (1.34)
  waiting for transfers between devices: 251 us -> 406 us
    psum x1 -> x2, waiting for transfers between devices: 149 us -> 261 us  [body(): summed = lax.psum(summed, axis_name=w)]
    unnamed x10 -> x11, waiting for transfers between devices: 85.8 us -> 126 us
    psum x1 -> x2, blocking collectives: 22.6 us -> 17.8 us  [body(): summed = lax.psum(summed, axis_name=w)]
    unnamed x117 -> x109, local copies, waits for them, and re-layouts: 34.8 us -> 33.4 us
  transfers between devices with their start and end apart: 10 -> 11, of which waited for: 8 -> 10; matrix products, arithmetic and copies ran while one was open for 13% -> 6% of each run, Pallas kernels for 0% -> 0%
where the time goes in v1:
time: 582 us; the launch traced here: 580 us
  waiting for transfers between devices  406 us (70%)
  blocking collectives  57.1 us (10%)
  local copies, waits for them, and re-layouts  45.1 us (8%)
  other arithmetic  23.3 us (4%)
  matrix products  22.9 us (4%)
  between operations  15.7 us (3%)
  starting transfers between devices  10.3 us (2%)
    psum x2, waiting for transfers between devices, body(): summed = lax.psum(summed, axis_name=w)  261 us
    unnamed x11, waiting for transfers between devices  126 us
    unnamed x109, local copies, waits for them, and re-layouts  33.4 us
    psum x2, blocking collectives, body(): summed = lax.psum(summed, axis_name=w)  17.8 us
  transfers between devices with their start and end apart: 11, of which 10 were waited for; matrix products, arithmetic and copies ran while one was open for 6% of the time, Pallas kernels for 0%

profile of v1, /device:TPU:0, one launch (start us, length us, event | category | flops | bytes accessed | tf_op | source)
XLA Modules:
  0.0 580.3 jit_solution(14251380701560206734)
XLA Ops:
  7.3 10.4 %all_gather.12 = bf16[1,512,768]{1,2,0:T(8,128)(2,1)S(1)} all-gather(bf16[1,512,192]{1,2,0:T(8,128)(2,1)} %param.8), channel_id=1, replica_groups=mesh['dp'=4,'seq'=2,'mp'=4] {'mp'}, dimensions={2}, use_global_device_ids=true | all-gather | bytes 983040 | tf_op jit(solution)/shard_map/all_gather | solution.py:174
  18.1 0.7 fusion.78
  18.9 1.0 copy-done.15
  20.0 0.9 fusion.85
  21.0 1.1 fusion.46
  22.1 0.7 pad_maximum_fusion.12
  22.8 4.1 collective-permute-start
  26.9 1.3 collective-permute-start.1
  28.4 1.1 fusion.81
  30.1 3.8 collective-permute-done.1
  33.9 1.2 pad_maximum_fusion.2
  38.6 2.7 copy.56
  43.2 41.0 %all-reduce.19.cloned.1.call-done = f32[1,512,768]{1,0,2:T(1,128)} async-done(((f32[1,512,768]{1,0,2:T(1,128)}), f32[1,512,768]{1,0,2:T(1,128)}) %all-reduce.19.cloned.1.call-update) | async-done | bytes 1572880
  84.2 2.1 dynamic-slice_add_fusion
  86.5 8.6 %all_gather.14 = bf16[1,512,768]{1,2,0:T(8,128)(2,1)} all-gather(bf16[1,512,192]{1,2,0:T(8,128)(2,1)S(1)} %copy-done.10), channel_id=1, replica_groups=mesh['dp'=4,'seq'=2,'mp'=4] {'mp'}, dimensions={2}, use_global_device_ids=true | all-gather | bytes 983040 | tf_op jit(solution)/shard_map/all_gather | solution.py:175
  95.1 11.2 %all-gather.2.cloned.1.call-done = f32[1,512,768]{1,0,2:T(1,128)} async-done(((f32[1,512,192]{1,0,2:T(1,128)}), f32[1,512,768]{1,0,2:T(1,128)}) %all-gather.2.cloned.1.call-update) | async-done | bytes 1572880 | tf_op jit(solution)/shard_map/all_gather | solution.py:204
  106.3 2.4 reduce_sum.111
  108.9 1.1 copy-done.4
  110.3 1.0 copy-done.20
  111.3 0.7 convolution_bitcast_fusion.2
  113.5 0.7 copy-done.38
  114.4 2.0 convolution_bitcast_fusion
  116.3 4.8 copy.60
  121.3 0.9 copy.63
  122.2 2.9 fusion.16
  125.1 1.9 fusion.48
  127.0 37.1 %all-reduce.21.cloned.1.call-done = f32[1,512,768]{1,0,2:T(1,128)} async-done(((f32[1,512,768]{1,0,2:T(1,128)}), f32[1,512,768]{1,0,2:T(1,128)}) %all-reduce.21.cloned.1.call-update) | async-done | bytes 1572880
  164.2 1.3 constant_dynamic-slice_fusion
  165.5 0.7 copy-done.5
  166.4 6.0 %all-reduce.9 = (f32[1,512,1]{1,2,0:T(1,128)S(1)}, f32[1,512,1]{1,2,0:T(1,128)S(1)}) all-reduce(f32[1,512,1]{1,2,0:T(1,128)S(1)} %bitcast.303, f32[1,512,1]{1,2,0:T(1,128)S(1)} %bitcast.304), channel_id=1, replica_groups=mesh['dp'=4,'seq'=2,'mp'=4] {'mp'}, use_global_device_ids=true, to_apply=%region_12.13 | all-reduce | flops 1024 | bytes 8192 | tf_op jit(solution)/shard_map/psum | solution.py:236
  172.4 1.2 fusion.98
  173.6 8.3 %all_gather.15 = bf16[1,512,768]{1,2,0:T(8,128)(2,1)S(1)} all-gather(bf16[1,512,192]{1,2,0:T(8,128)(2,1)S(1)} %fusion.98), channel_id=1, replica_groups=mesh['dp'=4,'seq'=2,'mp'=4] {'mp'}, dimensions={2}, use_global_device_ids=true | all-gather | bytes 983040 | tf_op jit(solution)/shard_map/all_gather | solution.py:246
  182.2 1.2 fusion.13
  183.5 0.7 reshape.839
  184.2 1.6 fusion.47
  185.9 2.1 convolution_bitcast_fusion.3
  192.3 3.4 collective-permute-start.2
  195.7 1.3 collective-permute-start.3
  198.3 4.1 collective-permute-done.3
  203.1 0.7 copy-done.37
  204.4 2.0 fusion.76
  206.4 2.9 fusion.6
  209.4 4.8 copy.86
  214.2 2.5 copy.151
  216.8 2.8 fusion.5
  219.6 4.8 copy.88
  224.4 2.5 copy.150
  227.0 104.4 %all-reduce.25.cloned.1.call-done = (f32[768,3,192]{0,2,1:T(8,128)}, f32[192,768]{1,0:T(8,128)}, f32[768,2,288]{0,2,1:T(8,128)}, f32[288,768]{1,0:T(8,128)}) async-done(((f32[768,3,192]{0,2,1:T(8,128)}, f32[192,768]{1,0:T(8,128)}, f32[768,2,288]{0,2,1:T(8,128)}, f32[288,768]{1,0:T(8,128)}), (f32[768,3,192]{0,2,1:T(8,128)}, f32[192,768]{1,0:T(8,128)}, f32[768,2,288]{0,2,1:T(8,128)}, ...) | async-done | bytes 5013520 | tf_op jit(solution)/shard_map/psum | solution.py:316
  331.5 1.4 fusion
  332.9 24.2 %reduce-scatter.7.cloned.1.call-done = bf16[192,512]{1,0:T(8,128)(2,1)} async-done(((bf16[768,512]{1,0:T(8,128)(2,1)}), bf16[192,512]{1,0:T(8,128)(2,1)}) %reduce-scatter.7.cloned.1.call-update) | async-done | bytes 196624
  357.1 1.4 fusion.44
  358.4 0.8 copy.79
  359.2 23.5 %reduce-scatter.9.cloned.1.call-done = bf16[192,512]{1,0:T(8,128)(2,1)} async-done(((bf16[768,512]{1,0:T(8,128)(2,1)}), bf16[192,512]{1,0:T(8,128)(2,1)}) %reduce-scatter.9.cloned.1.call-update) | async-done | bytes 196624
  382.7 1.1 reshape_bitcast_fusion
  383.8 1.2 fusion.37
  385.0 4.9 all-reduce.12
  389.9 12.9 %all-reduce.10 = (f32[192]{0:T(256)}, f32[192]{0:T(256)}) all-reduce(f32[192]{0:T(256)S(1)} %get-tuple-element.48, f32[192]{0:T(256)S(1)} %get-tuple-element.49), channel_id=1, replica_groups=mesh['dp'=4,'seq'=2,'mp'=4] {'dp'}, use_global_device_ids=true, to_apply=%region_29.30 | all-reduce | flops 384 | bytes 3072 | tf_op jit(solution)/shard_map/psum | solution.py:316
  402.8 6.0 %all-reduce.8 = (f32[1,512,1]{1,2,0:T(1,128)S(1)}, f32[1,512,1]{1,2,0:T(1,128)S(1)}) all-reduce(f32[1,512,1]{1,2,0:T(1,128)S(1)} %bitcast.299, f32[1,512,1]{1,2,0:T(1,128)S(1)} %bitcast.300), channel_id=1, replica_groups=mesh['dp'=4,'seq'=2,'mp'=4] {'mp'}, use_global_device_ids=true, to_apply=%region_18.19 | all-reduce | flops 1024 | bytes 8192 | tf_op jit(solution)/shard_map/psum | solution.py:289
  408.9 2.0 fusion.35
  410.9 156.1 %all-reduce.23.cloned.1.call-done = (f32[768,3,192]{0,2,1:T(8,128)}, f32[192,768]{1,0:T(8,128)}, f32[768,2,288]{0,2,1:T(8,128)}, f32[288,768]{1,0:T(8,128)}) async-done(((f32[768,3,192]{0,2,1:T(8,128)}, f32[192,768]{1,0:T(8,128)}, f32[768,2,288]{0,2,1:T(8,128)}, f32[288,768]{1,0:T(8,128)}), (f32[768,3,192]{0,2,1:T(8,128)}, f32[192,768]{1,0:T(8,128)}, f32[768,2,288]{0,2,1:T(8,128)}, ...) | async-done | bytes 5013520 | tf_op jit(solution)/shard_map/psum | solution.py:316
  567.0 2.9 copy.162
  570.0 0.8 copy.163
  570.8 1.2 copy.164
  572.6 0.9 copy.165
  (183 shorter events, 16.3 us)
Async XLA Ops:
  7.2 10.9 %copy-start = (bf16[768,3,192]{0,2,1:T(8,128)(2,1)S(1)}, bf16[768,3,192]{0,2,1:T(8,128)(2,1)}, u32[]{:S(2)}) copy-start(bf16[768,3,192]{0,2,1:T(8,128)(2,1)} %param.12) | copy-start | bytes 2654212
  7.2 10.9 %copy-start.43 = (f32[768]{0:T(1024)S(1)}, f32[768]{0:T(1024)}, u32[]{:S(2)}) copy-start(f32[768]{0:T(1024)} %param.10) | copy-start | bytes 9220
  7.2 77.0 %all-reduce.19.cloned.1.call-start = ((), (), s32[]{:S(2)}) async-start(), calls=%async_computation.5 | async-start | bytes 3145728
  18.8 1.0 copy-start.15
  20.9 1.9 copy-start.16
  22.8 7.3 %collective-permute-start = (bf16[1,64,384]{1,2,0:T(8,128)(2,1)}, bf16[1,64,384]{1,2,0:T(8,128)(2,1)}, u32[]{:S(2)}, u32[]{:S(2)}) collective-permute-start(bf16[1,64,384]{1,2,0:T(8,128)(2,1)} %get-tuple-element.77), channel_id=1, source_target_pairs={{0,4},{1,5},{2,6},{3,7},{8,12},{9,13},{10,14},{11,15},{16,20},{17,... | collective-permute-start | bytes 147464 | tf_op jit(solution)/shard_map/ppermute | solution.py:16
  26.9 7.0 %collective-permute-start.1 = (bf16[1,64,384]{1,2,0:T(8,128)(2,1)}, bf16[1,64,384]{1,2,0:T(8,128)(2,1)}, u32[]{:S(2)}, u32[]{:S(2)}) collective-permute-start(bf16[1,64,384]{1,2,0:T(8,128)(2,1)} %get-tuple-element.78), channel_id=1, source_target_pairs={{4,0},{5,1},{6,2},{7,3},{12,8},{13,9},{14,10},{15,11},{20,16},{21,... | collective-permute-start | bytes 147464 | tf_op jit(solution)/shard_map/ppermute | solution.py:19
  30.0 5.4 copy-start.22
  35.4 0.7 copy-start.25
  35.4 0.7 copy-start.27
  36.0 1.2 copy-start.1
  36.6 1.5 copy-start.18
  36.8 0.7 copy-start.29
  36.8 0.7 copy-start.31
  37.4 0.7 copy-start.13
  41.3 0.7 copy-start.45
  41.3 42.9 %copy-start.33 = (bf16[1,512,192]{1,2,0:T(8,128)(2,1)S(1)}, bf16[1,512,192]{1,2,0:T(8,128)(2,1)}, u32[]{:S(2)}) copy-start(bf16[1,512,192]{1,2,0:T(8,128)(2,1)} %param.8) | copy-start | bytes 589828
  41.3 45.1 %copy-start.10 = (bf16[1,512,192]{1,2,0:T(8,128)(2,1)S(1)}, bf16[1,512,192]{1,2,0:T(8,128)(2,1)}, u32[]{:S(2)}) copy-start(bf16[1,512,192]{1,2,0:T(8,128)(2,1)} %param.9) | copy-start | bytes 589828
  41.3 64.9 %all-gather.2.cloned.1.call-start = ((), (), s32[]{:S(2)}) async-start(), calls=%async_computation.2 | async-start | bytes 1966080 | tf_op jit(solution)/shard_map/all_gather | solution.py:204
  86.4 77.8 %all-reduce.21.cloned.1.call-start = ((), (), s32[]{:S(2)}) async-start(), calls=%async_computation.6 | async-start | bytes 3145728
  106.3 2.4 copy-start.3
  108.7 1.4 copy-start.4
  110.1 1.2 copy-start.20
  110.1 1.2 copy-start.42
  111.2 1.1 copy-start.7
  111.3 1.2 copy-start.44
  112.5 1.0 copy-start.8
  113.5 0.7 copy-start.38
  113.5 0.8 copy-start.40
  121.2 210.2 %all-reduce.25.cloned.1.call-start = ((), (), s32[]{:S(2)}) async-start(), calls=%async_computation.8 | async-start | bytes 10027008 | tf_op jit(solution)/shard_map/psum | solution.py:316
  121.2 3.9 copy-start.39
  121.2 3.9 copy-start.41
  127.0 45.3 %copy-start.11 = (bf16[1,512,192]{1,2,0:T(8,128)(2,1)S(1)}, bf16[1,512,192]{1,2,0:T(8,128)(2,1)}, u32[]{:S(2)}) copy-start(bf16[1,512,192]{1,2,0:T(8,128)(2,1)} %param.9) | copy-start | bytes 589828
  165.4 0.8 copy-start.5
  172.3 9.6 %copy-start.19 = (bf16[192,768]{1,0:T(8,128)(2,1)S(1)}, bf16[192,768]{1,0:T(8,128)(2,1)}, u32[]{:S(2)}) copy-start(bf16[192,768]{1,0:T(8,128)(2,1)} %param.13) | copy-start | bytes 884740
  172.3 9.9 %copy-start.14 = (bf16[1,4,128,3,64]{2,1,4,3,0:T(4,128)(2,1)S(1)}, bf16[1,4,128,3,64]{2,1,4,3,0:T(4,128)(2,1)}, u32[]{:S(2)}) copy-start(bf16[1,4,128,3,64]{2,1,4,3,0:T(4,128)(2,1)} %copy-done.13) | copy-start | bytes 589828
  184.2 3.8 copy-start.24
  185.9 2.2 copy-start.2
  185.9 2.2 copy-start.30
  185.9 2.2 copy-start.32
  188.1 0.9 copy-start.26
  188.1 1.0 copy-start.28
  188.1 1.4 copy-start.23
  192.3 5.9 %collective-permute-start.2 = (bf16[1,64,384]{1,2,0:T(8,128)(2,1)S(1)}, bf16[1,64,384]{1,2,0:T(8,128)(2,1)S(1)}, u32[]{:S(2)}, u32[]{:S(2)}) collective-permute-start(bf16[1,64,384]{1,2,0:T(8,128)(2,1)S(1)} %get-tuple-element.59), channel_id=1, source_target_pairs={{0,4},{1,5},{2,6},{3,7},{8,12},{9,13},{10,14},{11,15},{16,20},{17,... | collective-permute-start | bytes 147464 | tf_op jit(solution)/shard_map/ppermute | solution.py:16
  195.7 6.7 %collective-permute-start.3 = (bf16[1,64,384]{1,2,0:T(8,128)(2,1)S(1)}, bf16[1,64,384]{1,2,0:T(8,128)(2,1)S(1)}, u32[]{:S(2)}, u32[]{:S(2)}) collective-permute-start(bf16[1,64,384]{1,2,0:T(8,128)(2,1)S(1)} %get-tuple-element.60), channel_id=1, source_target_pairs={{4,0},{5,1},{6,2},{7,3},{12,8},{13,9},{14,10},{15,11},{20,16},{21,... | collective-permute-start | bytes 147464 | tf_op jit(solution)/shard_map/ppermute | solution.py:19
  203.0 0.9 copy-start.37
  203.0 1.0 copy-start.17
  204.3 2.1 copy-start.34
  204.3 2.1 copy-start.35
  206.4 150.7 %reduce-scatter.7.cloned.1.call-start = ((), (), s32[]{:S(2)}) async-start(), calls=%async_computation.3 | async-start | bytes 983040
  216.7 166.0 %reduce-scatter.9.cloned.1.call-start = ((), (), s32[]{:S(2)}) async-start(), calls=%async_computation.4 | async-start | bytes 983040
  226.9 340.1 %all-reduce.23.cloned.1.call-start = ((), (), s32[]{:S(2)}) async-start(), calls=%async_computation.7 | async-start | bytes 10027008 | tf_op jit(solution)/shard_map/psum | solution.py:316
  332.9 76.0 %copy-start.6 = (f32[1,512,192]{1,0,2:T(1,128)S(1)}, f32[1,512,192]{1,0,2:T(1,128)}, u32[]{:S(2)}) copy-start(f32[1,512,192]{1,0,2:T(1,128)} %copy-done.5) | copy-start | bytes 1179652
  332.9 76.0 %copy-start.12 = (bf16[1,512,192]{1,2,0:T(8,128)(2,1)S(1)}, bf16[1,512,192]{1,2,0:T(8,128)(2,1)}, u32[]{:S(2)}) copy-start(bf16[1,512,192]{1,2,0:T(8,128)(2,1)} %param.9) | copy-start | bytes 589828
  567.0 3.0 copy-start.36
  567.0 3.8 copy-start.9
  570.8 1.8 copy-start.21
Sparse Core Ops, SparseCore 0:
  41.5 42.7 all-reduce.18
  86.5 19.6 all-gather.1
  121.3 42.8 all-reduce.20
  206.5 124.8 all-reduce.24
  333.8 23.2 reduce-scatter.6
  359.4 23.2 reduce-scatter.8
  385.3 181.6 all-reduce.22
